TPU v7x, 32 devices: a whole 2x2x4 slice. The times are simulated.
32 devices in a mesh: member: 8 (over z, x), space: 4 (over y, core).
Axes of the slice: x: 2, y: 2, z: 4, core: 2. Of those that a mesh axis runs over, the one named last changes fastest.
Arguments:
- alpha: float32 [16, 16, 32, 1280], P('member', None, 'space'), may hold values from -6 to 6
- perturb: bfloat16 [4, 16, 16, 32, 1280], P(None, 'member', None, 'space'), may hold values from -1.5 to 1.5
- kappa: float32 [32, 1280], P('space'), may hold values from 0.1 to 0.24
- land: int32 [32, 1280], P('space'), may hold values 0 or 1
- obs_weight: float32 [4, 16, 32, 1280], P(None, 'member', 'space'), may hold values from 0.2 to 5
- innovation: float32 [4, 16, 32, 1280], P(None, 'member', 'space'), may hold values from -6 to 6
Outputs:
- gradient: float32 [16, 16, 32, 1280], P('member', None, 'space')
- weighted_misfit: float32 [4, 16, 32, 1280], P(None, 'member', 'space')
All inputs are finite; a program needn't handle non-finite values. No bound on the sum of `land` on one device may be relied on, other than what follows from the above.
Results may differ from a plain program's by a relative error of at most 0.0003.
Values sent between devices are 32-bit elements; how exact they have to be, the bound alone decides.
No kernel may reach another device: no remote copies, remote signals or barrier semaphores. Data moves between devices by JAX's collectives and lax.ppermute only.
A program may use at most 64 MiB of HBM per device.

v0:
```python
import jax
import jax.numpy as jnp
from jax import lax
from jax.sharding import PartitionSpec as P

STEPS = 4


def extended_2(cells, sides, width):
    for axis, dim in sides:
        count = lax.axis_size(axis)
        ends = count - 1
        head = lax.slice_in_dim(cells, 0, width, axis=dim)
        tail = lax.slice_in_dim(cells, cells.shape[dim] - width, cells.shape[dim], axis=dim)
        cells = jnp.concatenate(
            [
                lax.ppermute(tail, axis, [(i, (i + 1) % count) for i in range(ends)]),
                cells,
                lax.ppermute(head, axis, [((i + 1) % count, i) for i in range(ends)]),
            ],
            axis=dim,
        )
    return cells


def smooth_step(padded, coef_east, coef_west, coef_north, coef_south):
    middle = padded[:, :, 1:-1, :]
    return (
        middle
        + coef_east * (jnp.roll(middle, -1, axis=-1) - middle)
        + coef_west * (jnp.roll(middle, 1, axis=-1) - middle)
        + coef_north * (padded[:, :, 2:, :] - middle)
        + coef_south * (padded[:, :, :-2, :] - middle)
    )


def body(alpha, perturb, kappa, land, obs_weight, innovation):
    tile_rows = alpha.shape[2]
    extended = extended_2(kappa, (("space", 0),), STEPS + 1)
    inner = extended[1:-1]
    coef_north = 0.5 * (inner + extended[2:])
    coef_south = 0.5 * (inner + extended[:-2])
    coef_east = 0.5 * (inner + jnp.roll(inner, -1, axis=1))
    coef_west = 0.5 * (inner + jnp.roll(inner, 1, axis=1))

    def diffuse(field):
        current = field
        for sweep in range(STEPS):
            padded = extended_2(current, (("space", 2),), 1)
            current = smooth_step(
                padded,
                coef_east[STEPS : STEPS + tile_rows],
                coef_west[STEPS : STEPS + tile_rows],
                coef_north[STEPS : STEPS + tile_rows],
                coef_south[STEPS : STEPS + tile_rows],
            )
        return current

    sea = land.astype(jnp.float32)
    local = diffuse(alpha) * sea
    partial_sum = jnp.sum(perturb * local[None], axis=1)
    total = lax.psum(partial_sum, "member")
    weight_all, innov_all = (
        lax.all_gather(obs_weight, "member", axis=1, tiled=True),
        lax.all_gather(innovation, "member", axis=1, tiled=True),
    )
    whole_misfit = weight_all * (total - innov_all)
    own_width = obs_weight.shape[1]
    weighted_misfit = lax.dynamic_slice_in_dim(
        whole_misfit, lax.axis_index("member") * own_width, own_width, 1
    )
    back = jnp.sum(perturb * whole_misfit[:, None], axis=0)
    gradient = diffuse(back * sea) + alpha
    return (gradient, weighted_misfit)


def solution(mesh):
    placed = (
        P("member", None, "space", None),
        P(None, "member", None, "space", None),
        P("space", None),
        P("space", None),
        P(None, "member", "space", None),
        P(None, "member", "space", None),
    )
    return jax.shard_map(
        body,
        mesh=mesh,
        in_specs=placed,
        out_specs=(P("member", None, "space", None), P(None, "member", "space", None)),
        check_vma=False,
    )
```

profile of v0, /device:TPU:1, one launch (start us, length us, event | category | flops | bytes accessed | tf_op | source)
XLA Modules:
  0.0 342.5 jit_solution(4764403704498449764)
XLA Ops:
  7.2 0.9 fusion.116
  8.1 4.5 %collective-permute-start = (f32[5,1280]{1,0:T(8,128)S(1)}, f32[5,1280]{1,0:T(8,128)S(1)}, u32[]{:S(2)}, u32[]{:S(2)}) collective-permute-start(f32[5,1280]{1,0:T(8,128)S(1)} %get-tuple-element.61), channel_id=1, source_target_pairs={{0,1},{1,2},{2,3},{4,5},{5,6},{6,7},{8,9},{9,10},{10,11},{12,13},{... | collective-permute-start | bytes 76808 | tf_op jit(solution)/shard_map/ppermute | solution.py:17
  12.6 1.9 collective-permute-start.1
  14.6 2.1 fusion.113
  16.7 1.9 collective-permute-start.2
  18.7 3.8 %collective-permute-start.3 = (f32[2,16,1,1280]{3,1,2,0:T(8,128)S(1)}, f32[2,16,1,1280]{3,1,2,0:T(8,128)S(1)}, u32[]{:S(2)}, u32[]{:S(2)}) collective-permute-start(f32[2,16,1,1280]{3,1,2,0:T(8,128)S(1)} %copy.57), channel_id=1, source_target_pairs={{0,1},{1,2},{2,3},{4,5},{5,6},{6,7},{8,9},{9,10},{10,11},{12,13},{... | collective-permute-start | bytes 491528 | tf_op jit(solution)/shard_map/ppermute | solution.py:17
  23.5 1.2 collective-permute-done.3
  24.9 1.0 fusion.48
  26.5 1.9 collective-permute-start.4
  28.5 4.4 %collective-permute-start.5 = (f32[2,16,1,1280]{3,1,2,0:T(8,128)S(1)}, f32[2,16,1,1280]{3,1,2,0:T(8,128)S(1)}, u32[]{:S(2)}, u32[]{:S(2)}) collective-permute-start(f32[2,16,1,1280]{3,1,2,0:T(8,128)S(1)} %copy.30), channel_id=1, source_target_pairs={{0,1},{1,2},{2,3},{4,5},{5,6},{6,7},{8,9},{9,10},{10,11},{12,13},{... | collective-permute-start | bytes 491528 | tf_op jit(solution)/shard_map/ppermute | solution.py:17
  33.0 0.9 collective-permute-done.4
  34.1 1.0 collective-permute-done.5
  35.3 1.0 fusion.42
  37.0 1.9 collective-permute-start.6
  38.9 4.4 %collective-permute-start.7 = (f32[2,16,1,1280]{3,1,2,0:T(8,128)S(1)}, f32[2,16,1,1280]{3,1,2,0:T(8,128)S(1)}, u32[]{:S(2)}, u32[]{:S(2)}) collective-permute-start(f32[2,16,1,1280]{3,1,2,0:T(8,128)S(1)} %copy.34), channel_id=1, source_target_pairs={{0,1},{1,2},{2,3},{4,5},{5,6},{6,7},{8,9},{9,10},{10,11},{12,13},{... | collective-permute-start | bytes 491528 | tf_op jit(solution)/shard_map/ppermute | solution.py:17
  43.4 0.9 collective-permute-done.6
  44.5 1.0 collective-permute-done.7
  45.7 1.0 fusion.36
  47.4 1.9 collective-permute-start.8
  49.4 4.4 %collective-permute-start.9 = (f32[2,16,1,1280]{3,1,2,0:T(8,128)S(1)}, f32[2,16,1,1280]{3,1,2,0:T(8,128)S(1)}, u32[]{:S(2)}, u32[]{:S(2)}) collective-permute-start(f32[2,16,1,1280]{3,1,2,0:T(8,128)S(1)} %copy.38), channel_id=1, source_target_pairs={{0,1},{1,2},{2,3},{4,5},{5,6},{6,7},{8,9},{9,10},{10,11},{12,13},{... | collective-permute-start | bytes 491528 | tf_op jit(solution)/shard_map/ppermute | solution.py:17
  53.9 0.9 collective-permute-done.8
  55.0 1.0 collective-permute-done.9
  56.2 1.1 fusion.30
  57.9 2.1 fusion
  61.6 115.5 %all-reduce.2.cloned.1.call-done = f32[4,16,8,1280]{3,2,1,0:T(8,128)} async-done(((f32[4,16,8,1280]{3,2,1,0:T(8,128)}), f32[4,16,8,1280]{3,2,1,0:T(8,128)}) %all-reduce.2.cloned.1.call-update) | async-done | bytes 2621456 | tf_op jit(solution)/shard_map/psum | solution.py:62
  177.0 55.2 %all-gather.3.cloned.1.call-done = f32[4,16,8,1280]{3,2,1,0:T(8,128)} async-done(((f32[4,2,8,1280]{3,2,1,0:T(8,128)}), f32[4,16,8,1280]{3,2,1,0:T(8,128)}) %all-gather.3.cloned.1.call-update) | async-done | bytes 2621456 | tf_op jit(solution)/shard_map/all_gather | solution.py:64
  232.2 55.2 %all-gather.5.cloned.1.call-done = f32[4,16,8,1280]{3,2,1,0:T(8,128)} async-done(((f32[4,2,8,1280]{3,2,1,0:T(8,128)}), f32[4,16,8,1280]{3,2,1,0:T(8,128)}) %all-gather.5.cloned.1.call-update) | async-done | bytes 2621456 | tf_op jit(solution)/shard_map/all_gather | solution.py:65
  287.5 3.9 %subtract_multiply_fusion = f32[4,16,8,1280]{3,2,1,0:T(8,128)S(1)} fusion(f32[4,16,8,1280]{3,2,1,0:T(8,128)} %all-gather.3.cloned.1.call-done, f32[4,16,8,1280]{3,2,1,0:T(8,128)} %all-reduce.2.cloned.1.call-done, f32[4,16,8,1280]{3,2,1,0:T(8,128)} %all-gather.5.cloned.1.call-done), kind=kLoop, calls=%fused_computation.4 | loop fusion | flops 1310720 | bytes 10485760 | tf_op jit(solution)/shard_map/mul | solution.py:67
  292.8 4.2 %collective-permute-start.10 = (f32[2,16,1,1280]{3,1,2,0:T(8,128)S(1)}, f32[2,16,1,1280]{3,1,2,0:T(8,128)S(1)}, u32[]{:S(2)}, u32[]{:S(2)}) collective-permute-start(f32[2,16,1,1280]{3,1,2,0:T(8,128)S(1)} %copy.40), channel_id=1, source_target_pairs={{1,0},{2,1},{3,2},{5,4},{6,5},{7,6},{9,8},{10,9},{11,10},{13,12},{... | collective-permute-start | bytes 491528 | tf_op jit(solution)/shard_map/ppermute | solution.py:19
  297.0 3.0 collective-permute-start.11
  300.0 0.8 constant_dynamic-slice_fusion
  301.3 1.0 collective-permute-done.11
  302.5 1.0 fusion.23
  304.1 1.9 collective-permute-start.12
  306.1 4.4 %collective-permute-start.13 = (f32[2,16,1,1280]{3,1,2,0:T(8,128)S(1)}, f32[2,16,1,1280]{3,1,2,0:T(8,128)S(1)}, u32[]{:S(2)}, u32[]{:S(2)}) collective-permute-start(f32[2,16,1,1280]{3,1,2,0:T(8,128)S(1)} %copy.46), channel_id=1, source_target_pairs={{0,1},{1,2},{2,3},{4,5},{5,6},{6,7},{8,9},{9,10},{10,11},{12,13},{... | collective-permute-start | bytes 491528 | tf_op jit(solution)/shard_map/ppermute | solution.py:17
  310.6 0.9 collective-permute-done.12
  311.7 1.0 collective-permute-done.13
  312.9 1.0 fusion.17
  314.6 1.9 collective-permute-start.14
  316.5 4.4 %collective-permute-start.15 = (f32[2,16,1,1280]{3,1,2,0:T(8,128)S(1)}, f32[2,16,1,1280]{3,1,2,0:T(8,128)S(1)}, u32[]{:S(2)}, u32[]{:S(2)}) collective-permute-start(f32[2,16,1,1280]{3,1,2,0:T(8,128)S(1)} %copy.50), channel_id=1, source_target_pairs={{0,1},{1,2},{2,3},{4,5},{5,6},{6,7},{8,9},{9,10},{10,11},{12,13},{... | collective-permute-start | bytes 491528 | tf_op jit(solution)/shard_map/ppermute | solution.py:17
  321.0 0.9 collective-permute-done.14
  322.1 1.0 collective-permute-done.15
  323.3 1.1 fusion.11
  325.1 1.9 collective-permute-start.16
  327.0 4.4 %collective-permute-start.17 = (f32[2,16,1,1280]{3,1,2,0:T(8,128)S(1)}, f32[2,16,1,1280]{3,1,2,0:T(8,128)S(1)}, u32[]{:S(2)}, u32[]{:S(2)}) collective-permute-start(f32[2,16,1,1280]{3,1,2,0:T(8,128)S(1)} %copy.54), channel_id=1, source_target_pairs={{0,1},{1,2},{2,3},{4,5},{5,6},{6,7},{8,9},{9,10},{10,11},{12,13},{... | collective-permute-start | bytes 491528 | tf_op jit(solution)/shard_map/ppermute | solution.py:17
  331.5 0.9 collective-permute-done.16
  332.6 1.0 collective-permute-done.17
  333.8 2.2 fusion.5
  (82 shorter events, 11.8 us)
Async XLA Ops:
  7.2 15.3 %copy-start = (f32[2,16,8,1280]{3,2,1,0:T(8,128)S(1)}, f32[2,16,8,1280]{3,2,1,0:T(8,128)}, u32[]{:S(2)}) copy-start(f32[2,16,8,1280]{3,2,1,0:T(8,128)} %param.6) | copy-start | bytes 3932164
  7.2 169.9 %all-reduce.2.cloned.1.call-start = ((), (), s32[]{:S(2)}) async-start(), calls=%async_computation.1 | async-start | bytes 5242880 | tf_op jit(solution)/shard_map/psum | solution.py:62
  8.1 14.9 %collective-permute-start = (f32[5,1280]{1,0:T(8,128)S(1)}, f32[5,1280]{1,0:T(8,128)S(1)}, u32[]{:S(2)}, u32[]{:S(2)}) collective-permute-start(f32[5,1280]{1,0:T(8,128)S(1)} %get-tuple-element.61), channel_id=1, source_target_pairs={{0,1},{1,2},{2,3},{4,5},{5,6},{6,7},{8,9},{9,10},{10,11},{12,13},{... | collective-permute-start | bytes 76808 | tf_op jit(solution)/shard_map/ppermute | solution.py:17
  12.6 10.4 %collective-permute-start.1 = (f32[5,1280]{1,0:T(8,128)S(1)}, f32[5,1280]{1,0:T(8,128)S(1)}, u32[]{:S(2)}, u32[]{:S(2)}) collective-permute-start(f32[5,1280]{1,0:T(8,128)S(1)} %get-tuple-element.62), channel_id=1, source_target_pairs={{1,0},{2,1},{3,2},{5,4},{6,5},{7,6},{9,8},{10,9},{11,10},{13,12},{... | collective-permute-start | bytes 76808 | tf_op jit(solution)/shard_map/ppermute | solution.py:19
  16.7 6.6 %collective-permute-start.2 = (f32[2,16,1,1280]{3,1,2,0:T(8,128)S(1)}, f32[2,16,1,1280]{3,1,2,0:T(8,128)S(1)}, u32[]{:S(2)}, u32[]{:S(2)}) collective-permute-start(f32[2,16,1,1280]{3,1,2,0:T(8,128)S(1)} %copy.56), channel_id=1, source_target_pairs={{1,0},{2,1},{3,2},{5,4},{6,5},{7,6},{9,8},{10,9},{11,10},{13,12},{... | collective-permute-start | bytes 491528 | tf_op jit(solution)/shard_map/ppermute | solution.py:19
  18.6 4.3 %copy-start.4 = (s32[8,1280]{1,0:T(8,128)S(1)}, s32[8,1280]{1,0:T(8,128)}, u32[]{:S(2)}) copy-start(s32[8,1280]{1,0:T(8,128)} %param.9) | copy-start | bytes 122884
  18.6 4.4 %copy-start.3 = (f32[8,1280]{1,0:T(8,128)S(1)}, f32[8,1280]{1,0:T(8,128)}, u32[]{:S(2)}) copy-start(f32[8,1280]{1,0:T(8,128)} %param.8) | copy-start | bytes 122884
  18.7 6.0 %collective-permute-start.3 = (f32[2,16,1,1280]{3,1,2,0:T(8,128)S(1)}, f32[2,16,1,1280]{3,1,2,0:T(8,128)S(1)}, u32[]{:S(2)}, u32[]{:S(2)}) collective-permute-start(f32[2,16,1,1280]{3,1,2,0:T(8,128)S(1)} %copy.57), channel_id=1, source_target_pairs={{0,1},{1,2},{2,3},{4,5},{5,6},{6,7},{8,9},{9,10},{10,11},{12,13},{... | collective-permute-start | bytes 491528 | tf_op jit(solution)/shard_map/ppermute | solution.py:17
  26.5 7.4 %collective-permute-start.4 = (f32[2,16,1,1280]{3,1,2,0:T(8,128)S(1)}, f32[2,16,1,1280]{3,1,2,0:T(8,128)S(1)}, u32[]{:S(2)}, u32[]{:S(2)}) collective-permute-start(f32[2,16,1,1280]{3,1,2,0:T(8,128)S(1)} %copy.28), channel_id=1, source_target_pairs={{1,0},{2,1},{3,2},{5,4},{6,5},{7,6},{9,8},{10,9},{11,10},{13,12},{... | collective-permute-start | bytes 491528 | tf_op jit(solution)/shard_map/ppermute | solution.py:19
  28.5 6.6 %collective-permute-start.5 = (f32[2,16,1,1280]{3,1,2,0:T(8,128)S(1)}, f32[2,16,1,1280]{3,1,2,0:T(8,128)S(1)}, u32[]{:S(2)}, u32[]{:S(2)}) collective-permute-start(f32[2,16,1,1280]{3,1,2,0:T(8,128)S(1)} %copy.30), channel_id=1, source_target_pairs={{0,1},{1,2},{2,3},{4,5},{5,6},{6,7},{8,9},{9,10},{10,11},{12,13},{... | collective-permute-start | bytes 491528 | tf_op jit(solution)/shard_map/ppermute | solution.py:17
  37.0 7.4 %collective-permute-start.6 = (f32[2,16,1,1280]{3,1,2,0:T(8,128)S(1)}, f32[2,16,1,1280]{3,1,2,0:T(8,128)S(1)}, u32[]{:S(2)}, u32[]{:S(2)}) collective-permute-start(f32[2,16,1,1280]{3,1,2,0:T(8,128)S(1)} %copy.32), channel_id=1, source_target_pairs={{1,0},{2,1},{3,2},{5,4},{6,5},{7,6},{9,8},{10,9},{11,10},{13,12},{... | collective-permute-start | bytes 491528 | tf_op jit(solution)/shard_map/ppermute | solution.py:19
  38.9 6.6 %collective-permute-start.7 = (f32[2,16,1,1280]{3,1,2,0:T(8,128)S(1)}, f32[2,16,1,1280]{3,1,2,0:T(8,128)S(1)}, u32[]{:S(2)}, u32[]{:S(2)}) collective-permute-start(f32[2,16,1,1280]{3,1,2,0:T(8,128)S(1)} %copy.34), channel_id=1, source_target_pairs={{0,1},{1,2},{2,3},{4,5},{5,6},{6,7},{8,9},{9,10},{10,11},{12,13},{... | collective-permute-start | bytes 491528 | tf_op jit(solution)/shard_map/ppermute | solution.py:17
  47.4 7.4 %collective-permute-start.8 = (f32[2,16,1,1280]{3,1,2,0:T(8,128)S(1)}, f32[2,16,1,1280]{3,1,2,0:T(8,128)S(1)}, u32[]{:S(2)}, u32[]{:S(2)}) collective-permute-start(f32[2,16,1,1280]{3,1,2,0:T(8,128)S(1)} %copy.36), channel_id=1, source_target_pairs={{1,0},{2,1},{3,2},{5,4},{6,5},{7,6},{9,8},{10,9},{11,10},{13,12},{... | collective-permute-start | bytes 491528 | tf_op jit(solution)/shard_map/ppermute | solution.py:19
  49.4 6.6 %collective-permute-start.9 = (f32[2,16,1,1280]{3,1,2,0:T(8,128)S(1)}, f32[2,16,1,1280]{3,1,2,0:T(8,128)S(1)}, u32[]{:S(2)}, u32[]{:S(2)}) collective-permute-start(f32[2,16,1,1280]{3,1,2,0:T(8,128)S(1)} %copy.38), channel_id=1, source_target_pairs={{0,1},{1,2},{2,3},{4,5},{5,6},{6,7},{8,9},{9,10},{10,11},{12,13},{... | collective-permute-start | bytes 491528 | tf_op jit(solution)/shard_map/ppermute | solution.py:17
  56.2 1.7 copy-start.1
  60.1 172.1 %all-gather.3.cloned.1.call-start = ((), (), s32[]{:S(2)}) async-start(), calls=%async_computation | async-start | bytes 2949120 | tf_op jit(solution)/shard_map/all_gather | solution.py:64
  60.9 226.6 %all-gather.5.cloned.1.call-start = ((), (), s32[]{:S(2)}) async-start(), calls=%async_computation.2 | async-start | bytes 2949120 | tf_op jit(solution)/shard_map/all_gather | solution.py:65
  287.5 4.0 %copy-start.2 = (bf16[4,2,16,8,1280]{4,3,2,1,0:T(8,128)(2,1)S(1)}, bf16[4,2,16,8,1280]{4,3,2,1,0:T(8,128)(2,1)}, u32[]{:S(2)}) copy-start(bf16[4,2,16,8,1280]{4,3,2,1,0:T(8,128)(2,1)} %param.7) | copy-start | bytes 7864324
  292.8 8.2 %collective-permute-start.10 = (f32[2,16,1,1280]{3,1,2,0:T(8,128)S(1)}, f32[2,16,1,1280]{3,1,2,0:T(8,128)S(1)}, u32[]{:S(2)}, u32[]{:S(2)}) collective-permute-start(f32[2,16,1,1280]{3,1,2,0:T(8,128)S(1)} %copy.40), channel_id=1, source_target_pairs={{1,0},{2,1},{3,2},{5,4},{6,5},{7,6},{9,8},{10,9},{11,10},{13,12},{... | collective-permute-start | bytes 491528 | tf_op jit(solution)/shard_map/ppermute | solution.py:19
  297.0 5.2 %collective-permute-start.11 = (f32[2,16,1,1280]{3,1,2,0:T(8,128)S(1)}, f32[2,16,1,1280]{3,1,2,0:T(8,128)S(1)}, u32[]{:S(2)}, u32[]{:S(2)}) collective-permute-start(f32[2,16,1,1280]{3,1,2,0:T(8,128)S(1)} %copy.42), channel_id=1, source_target_pairs={{0,1},{1,2},{2,3},{4,5},{5,6},{6,7},{8,9},{9,10},{10,11},{12,13},{... | collective-permute-start | bytes 491528 | tf_op jit(solution)/shard_map/ppermute | solution.py:17
  304.1 7.4 %collective-permute-start.12 = (f32[2,16,1,1280]{3,1,2,0:T(8,128)S(1)}, f32[2,16,1,1280]{3,1,2,0:T(8,128)S(1)}, u32[]{:S(2)}, u32[]{:S(2)}) collective-permute-start(f32[2,16,1,1280]{3,1,2,0:T(8,128)S(1)} %copy.44), channel_id=1, source_target_pairs={{1,0},{2,1},{3,2},{5,4},{6,5},{7,6},{9,8},{10,9},{11,10},{13,12},{... | collective-permute-start | bytes 491528 | tf_op jit(solution)/shard_map/ppermute | solution.py:19
  306.1 6.6 %collective-permute-start.13 = (f32[2,16,1,1280]{3,1,2,0:T(8,128)S(1)}, f32[2,16,1,1280]{3,1,2,0:T(8,128)S(1)}, u32[]{:S(2)}, u32[]{:S(2)}) collective-permute-start(f32[2,16,1,1280]{3,1,2,0:T(8,128)S(1)} %copy.46), channel_id=1, source_target_pairs={{0,1},{1,2},{2,3},{4,5},{5,6},{6,7},{8,9},{9,10},{10,11},{12,13},{... | collective-permute-start | bytes 491528 | tf_op jit(solution)/shard_map/ppermute | solution.py:17
  314.6 7.4 %collective-permute-start.14 = (f32[2,16,1,1280]{3,1,2,0:T(8,128)S(1)}, f32[2,16,1,1280]{3,1,2,0:T(8,128)S(1)}, u32[]{:S(2)}, u32[]{:S(2)}) collective-permute-start(f32[2,16,1,1280]{3,1,2,0:T(8,128)S(1)} %copy.48), channel_id=1, source_target_pairs={{1,0},{2,1},{3,2},{5,4},{6,5},{7,6},{9,8},{10,9},{11,10},{13,12},{... | collective-permute-start | bytes 491528 | tf_op jit(solution)/shard_map/ppermute | solution.py:19
  316.5 6.6 %collective-permute-start.15 = (f32[2,16,1,1280]{3,1,2,0:T(8,128)S(1)}, f32[2,16,1,1280]{3,1,2,0:T(8,128)S(1)}, u32[]{:S(2)}, u32[]{:S(2)}) collective-permute-start(f32[2,16,1,1280]{3,1,2,0:T(8,128)S(1)} %copy.50), channel_id=1, source_target_pairs={{0,1},{1,2},{2,3},{4,5},{5,6},{6,7},{8,9},{9,10},{10,11},{12,13},{... | collective-permute-start | bytes 491528 | tf_op jit(solution)/shard_map/ppermute | solution.py:17
  325.1 7.4 %collective-permute-start.16 = (f32[2,16,1,1280]{3,1,2,0:T(8,128)S(1)}, f32[2,16,1,1280]{3,1,2,0:T(8,128)S(1)}, u32[]{:S(2)}, u32[]{:S(2)}) collective-permute-start(f32[2,16,1,1280]{3,1,2,0:T(8,128)S(1)} %copy.52), channel_id=1, source_target_pairs={{1,0},{2,1},{3,2},{5,4},{6,5},{7,6},{9,8},{10,9},{11,10},{13,12},{... | collective-permute-start | bytes 491528 | tf_op jit(solution)/shard_map/ppermute | solution.py:19
  327.0 6.6 %collective-permute-start.17 = (f32[2,16,1,1280]{3,1,2,0:T(8,128)S(1)}, f32[2,16,1,1280]{3,1,2,0:T(8,128)S(1)}, u32[]{:S(2)}, u32[]{:S(2)}) collective-permute-start(f32[2,16,1,1280]{3,1,2,0:T(8,128)S(1)} %copy.54), channel_id=1, source_target_pairs={{0,1},{1,2},{2,3},{4,5},{5,6},{6,7},{8,9},{9,10},{10,11},{12,13},{... | collective-permute-start | bytes 491528 | tf_op jit(solution)/shard_map/ppermute | solution.py:17
Sparse Core Ops, SparseCore 0:
  60.2 116.7 all-reduce.1
  179.2 52.9 all-gather.2
  234.4 52.9 all-gather.4
where the time goes:
time: 343 us
  waiting for transfers between devices  241 us (70%)
  starting transfers between devices  57.5 us (17%)
  other arithmetic  16.3 us (5%)
  between operations  14.4 us (4%)
  local copies, waits for them, and re-layouts  13.1 us (4%)
    psum x1, waiting for transfers between devices, body(): total = lax.psum(partial_sum, 'member')  115 us
    all_gather x1, waiting for transfers between devices, body(): lax.all_gather(innovation, 'member', axis=1, tiled=True)  55.2 us
    all_gather x1, waiting for transfers between devices, body(): lax.all_gather(obs_weight, 'member', axis=1, tiled=True)  55.2 us
    ppermute x9, starting transfers between devices, extended_2(): lax.ppermute(tail, axis, [(i, (i + 1) % count) for i in range(ends)])  37.6 us
    ppermute x9, starting transfers between devices, extended_2(): lax.ppermute(head, axis, [((i + 1) % count, i) for i in range(ends)])  19.5 us
    ppermute x9, waiting for transfers between devices, extended_2(): lax.ppermute(tail, axis, [(i, (i + 1) % count) for i in range(ends)])  8.39 us
  transfers between devices with their start and end apart: 21, of which 19 were waited for; matrix products, arithmetic and copies ran while one was open for 2% of the time, Pallas kernels for 0%

commit v1 on v0

--- a/solution.py
+++ b/solution.py
@@ -4,6 +4,14 @@
 from jax.sharding import PartitionSpec as P
 
 STEPS = 4
+
+
+def doubling_sum(x, axis):
+    devices, result = (lax.axis_size(axis), x)
+    for stride in [1 << k for k in range(devices.bit_length() - 1)]:
+        pairs = [(i, i ^ stride) for i in range(devices)]
+        result = result + lax.ppermute(result, axis, pairs)
+    return result
 
 
 def extended_2(cells, sides, width):
@@ -59,7 +67,7 @@
     sea = land.astype(jnp.float32)
     local = diffuse(alpha) * sea
     partial_sum = jnp.sum(perturb * local[None], axis=1)
-    total = lax.psum(partial_sum, "member")
+    total = doubling_sum(partial_sum, "member")
     weight_all, innov_all = (
         lax.all_gather(obs_weight, "member", axis=1, tiled=True),
         lax.all_gather(innovation, "member", axis=1, tiled=True),

time: 343 us -> 390 us (1.14)
  waiting for transfers between devices: 241 us -> 279 us
  other arithmetic: 16.3 us -> 22 us
    ppermute x0 -> x3, waiting for transfers between devices: none -> 265 us  [doubling_sum(): result = result + lax.ppermute(result, axis, pairs)]
    psum x1 -> x0, waiting for transfers between devices: 115 us -> none  [body(): total = lax.psum(partial_sum, 'member')]
    all_gather x1, waiting for transfers between devices: 55.2 us -> 0.01 us  [body(): lax.all_gather(innovation, 'member', axis=1, tiled=True)]
    all_gather x1, waiting for transfers between devices: 55.2 us -> 0.01 us  [body(): lax.all_gather(obs_weight, 'member', axis=1, tiled=True)]
    add x0 -> x2, other arithmetic: none -> 6.33 us  [doubling_sum(): result = result + lax.ppermute(result, axis, pairs)]
    ppermute x0 -> x3, starting transfers between devices: none -> 4.59 us  [doubling_sum(): result = result + lax.ppermute(result, axis, pairs)]
  transfers between devices with their start and end apart: 21 -> 23, of which waited for: 19 -> 18; matrix products, arithmetic and copies ran while one was open for 2% -> 5% of each run, Pallas kernels for 0% -> 0%
where the time goes in v1:
time: 390 us; the launch traced here: 389 us
  waiting for transfers between devices  279 us (72%)
  starting transfers between devices  60.5 us (16%)
  other arithmetic  22 us (6%)
  between operations  14.7 us (4%)
  local copies, waits for them, and re-layouts  13 us (3%)
    ppermute x3, waiting for transfers between devices, doubling_sum(): result = result + lax.ppermute(result, axis, pairs)  265 us
    ppermute x9, starting transfers between devices, extended_2(): lax.ppermute(tail, axis, [(i, (i + 1) % count) for i in range(ends)])  37.1 us
    ppermute x9, starting transfers between devices, extended_2(): lax.ppermute(head, axis, [((i + 1) % count, i) for i in range(ends)])  18.7 us
  transfers between devices with their start and end apart: 23, of which 18 were waited for; matrix products, arithmetic and copies ran while one was open for 5% of the time, Pallas kernels for 0%

profile of v1, /device:TPU:1, one launch (start us, length us, event | category | flops | bytes accessed | tf_op | source)
XLA Modules:
  0.0 389.2 jit_solution(5337938806963436188)
XLA Ops:
  7.2 0.9 fusion.116
  8.1 4.5 %collective-permute-start = (f32[5,1280]{1,0:T(8,128)S(1)}, f32[5,1280]{1,0:T(8,128)S(1)}, u32[]{:S(2)}, u32[]{:S(2)}) collective-permute-start(f32[5,1280]{1,0:T(8,128)S(1)} %get-tuple-element.61), channel_id=1, source_target_pairs={{0,1},{1,2},{2,3},{4,5},{5,6},{6,7},{8,9},{9,10},{10,11},{12,13},{... | collective-permute-start | bytes 76808 | tf_op jit(solution)/shard_map/ppermute | solution.py:25
  12.6 1.9 collective-permute-start.1
  14.6 2.0 fusion.113
  16.6 1.9 collective-permute-start.2
  18.6 3.6 collective-permute-start.3
  23.5 1.0 collective-permute-done.3
  24.6 1.0 fusion.48
  26.3 1.9 collective-permute-start.4
  28.3 4.4 %collective-permute-start.5 = (f32[2,16,1,1280]{3,1,2,0:T(8,128)S(1)}, f32[2,16,1,1280]{3,1,2,0:T(8,128)S(1)}, u32[]{:S(2)}, u32[]{:S(2)}) collective-permute-start(f32[2,16,1,1280]{3,1,2,0:T(8,128)S(1)} %copy.30), channel_id=1, source_target_pairs={{0,1},{1,2},{2,3},{4,5},{5,6},{6,7},{8,9},{9,10},{10,11},{12,13},{... | collective-permute-start | bytes 491528 | tf_op jit(solution)/shard_map/ppermute | solution.py:25
  32.7 1.3 collective-permute-done.4
  35.1 1.0 fusion.42
  36.7 1.9 collective-permute-start.6
  38.7 4.4 %collective-permute-start.7 = (f32[2,16,1,1280]{3,1,2,0:T(8,128)S(1)}, f32[2,16,1,1280]{3,1,2,0:T(8,128)S(1)}, u32[]{:S(2)}, u32[]{:S(2)}) collective-permute-start(f32[2,16,1,1280]{3,1,2,0:T(8,128)S(1)} %copy.34), channel_id=1, source_target_pairs={{0,1},{1,2},{2,3},{4,5},{5,6},{6,7},{8,9},{9,10},{10,11},{12,13},{... | collective-permute-start | bytes 491528 | tf_op jit(solution)/shard_map/ppermute | solution.py:25
  43.2 1.3 collective-permute-done.6
  45.5 1.0 fusion.36
  47.2 1.9 collective-permute-start.8
  49.1 4.6 %collective-permute-start.9 = (f32[2,16,1,1280]{3,1,2,0:T(8,128)S(1)}, f32[2,16,1,1280]{3,1,2,0:T(8,128)S(1)}, u32[]{:S(2)}, u32[]{:S(2)}) collective-permute-start(f32[2,16,1,1280]{3,1,2,0:T(8,128)S(1)} %copy.38), channel_id=1, source_target_pairs={{0,1},{1,2},{2,3},{4,5},{5,6},{6,7},{8,9},{9,10},{10,11},{12,13},{... | collective-permute-start | bytes 491528 | tf_op jit(solution)/shard_map/ppermute | solution.py:25
  53.8 1.2 collective-permute-done.8
  56.0 1.1 fusion.30
  58.3 1.3 collective-permute-start.10
  59.6 62.9 %collective-permute-done.10 = f32[4,16,8,1280]{3,2,1,0:T(8,128)S(1)} collective-permute-done((f32[4,16,8,1280]{3,2,1,0:T(8,128)S(1)}, f32[4,16,8,1280]{3,2,1,0:T(8,128)S(1)}, u32[]{:S(2)}, u32[]{:S(2)}) %collective-permute-start.10) | collective-permute-done | bytes 2621472 | tf_op jit(solution)/shard_map/ppermute | solution.py:13
  122.5 1.9 add.143
  124.4 1.2 collective-permute-start.11
  125.6 89.3 %collective-permute-done.11 = f32[4,16,8,1280]{3,2,1,0:T(8,128)} collective-permute-done((f32[4,16,8,1280]{3,2,1,0:T(8,128)}, f32[4,16,8,1280]{3,2,1,0:T(8,128)}, u32[]{:S(2)}, u32[]{:S(2)}) %collective-permute-start.11) | collective-permute-done | bytes 2621472 | tf_op jit(solution)/shard_map/ppermute | solution.py:13
  214.9 4.4 %add.144 = f32[4,16,8,1280]{3,2,1,0:T(8,128)} add(f32[4,16,8,1280]{3,2,1,0:T(8,128)} %add.143, f32[4,16,8,1280]{3,2,1,0:T(8,128)} %collective-permute-done.11) | non-fusion elementwise | flops 655360 | bytes 7864320 | tf_op jit(solution)/shard_map/add | solution.py:13
  219.4 2.1 collective-permute-start.12
  221.5 113.1 %collective-permute-done.12 = f32[4,16,8,1280]{3,2,1,0:T(8,128)} collective-permute-done((f32[4,16,8,1280]{3,2,1,0:T(8,128)}, f32[4,16,8,1280]{3,2,1,0:T(8,128)}, u32[]{:S(2)}, u32[]{:S(2)}) %collective-permute-start.12) | collective-permute-done | bytes 2621472 | tf_op jit(solution)/shard_map/ppermute | solution.py:13
  334.6 4.8 %subtract_multiply_fusion = f32[4,16,8,1280]{3,2,1,0:T(8,128)S(1)} fusion(f32[4,16,8,1280]{3,2,1,0:T(8,128)} %all-gather.3.cloned.1.call-done, f32[4,16,8,1280]{3,2,1,0:T(8,128)} %all-gather.5.cloned.1.call-done, f32[4,16,8,1280]{3,2,1,0:T(8,128)} %add.144, f32[4,16,8,1280]{3,2,1,0:T(8,128)} %collective-permute-done.12), kind=kLoop, calls=%fused_computation.4 | loop fusion | flops 1966080 | bytes 13107200 | tf_op jit(solution)/shard_map/mul | solution.py:75
  340.8 3.3 collective-permute-start.13
  344.2 2.2 collective-permute-start.14
  346.4 0.8 constant_dynamic-slice_fusion
  347.6 1.0 collective-permute-done.14
  348.8 1.0 fusion.23
  350.5 1.9 collective-permute-start.15
  352.5 4.4 %collective-permute-start.16 = (f32[2,16,1,1280]{3,1,2,0:T(8,128)S(1)}, f32[2,16,1,1280]{3,1,2,0:T(8,128)S(1)}, u32[]{:S(2)}, u32[]{:S(2)}) collective-permute-start(f32[2,16,1,1280]{3,1,2,0:T(8,128)S(1)} %copy.46), channel_id=1, source_target_pairs={{0,1},{1,2},{2,3},{4,5},{5,6},{6,7},{8,9},{9,10},{10,11},{12,13},{... | collective-permute-start | bytes 491528 | tf_op jit(solution)/shard_map/ppermute | solution.py:25
  357.0 0.9 collective-permute-done.15
  358.1 1.0 collective-permute-done.16
  359.3 1.0 fusion.17
  360.9 1.9 collective-permute-start.17
  362.9 4.6 %collective-permute-start.18 = (f32[2,16,1,1280]{3,1,2,0:T(8,128)S(1)}, f32[2,16,1,1280]{3,1,2,0:T(8,128)S(1)}, u32[]{:S(2)}, u32[]{:S(2)}) collective-permute-start(f32[2,16,1,1280]{3,1,2,0:T(8,128)S(1)} %copy.50), channel_id=1, source_target_pairs={{0,1},{1,2},{2,3},{4,5},{5,6},{6,7},{8,9},{9,10},{10,11},{12,13},{... | collective-permute-start | bytes 491528 | tf_op jit(solution)/shard_map/ppermute | solution.py:25
  368.5 1.0 collective-permute-done.18
  369.7 1.1 fusion.11
  371.4 1.9 collective-permute-start.19
  373.4 4.4 %collective-permute-start.20 = (f32[2,16,1,1280]{3,1,2,0:T(8,128)S(1)}, f32[2,16,1,1280]{3,1,2,0:T(8,128)S(1)}, u32[]{:S(2)}, u32[]{:S(2)}) collective-permute-start(f32[2,16,1,1280]{3,1,2,0:T(8,128)S(1)} %copy.54), channel_id=1, source_target_pairs={{0,1},{1,2},{2,3},{4,5},{5,6},{6,7},{8,9},{9,10},{10,11},{12,13},{... | collective-permute-start | bytes 491528 | tf_op jit(solution)/shard_map/ppermute | solution.py:25
  377.9 0.9 collective-permute-done.19
  379.0 1.0 collective-permute-done.20
  380.2 2.2 fusion.5
  (87 shorter events, 13.7 us)
Async XLA Ops:
  7.2 15.1 %copy-start = (f32[2,16,8,1280]{3,2,1,0:T(8,128)S(1)}, f32[2,16,8,1280]{3,2,1,0:T(8,128)}, u32[]{:S(2)}) copy-start(f32[2,16,8,1280]{3,2,1,0:T(8,128)} %param.6) | copy-start | bytes 3932164
  7.2 214.3 %all-gather.3.cloned.1.call-start = ((), (), s32[]{:S(2)}) async-start(), calls=%async_computation | async-start | bytes 2949120 | tf_op jit(solution)/shard_map/all_gather | solution.py:72
  8.1 14.9 %collective-permute-start = (f32[5,1280]{1,0:T(8,128)S(1)}, f32[5,1280]{1,0:T(8,128)S(1)}, u32[]{:S(2)}, u32[]{:S(2)}) collective-permute-start(f32[5,1280]{1,0:T(8,128)S(1)} %get-tuple-element.61), channel_id=1, source_target_pairs={{0,1},{1,2},{2,3},{4,5},{5,6},{6,7},{8,9},{9,10},{10,11},{12,13},{... | collective-permute-start | bytes 76808 | tf_op jit(solution)/shard_map/ppermute | solution.py:25
  12.6 10.4 %collective-permute-start.1 = (f32[5,1280]{1,0:T(8,128)S(1)}, f32[5,1280]{1,0:T(8,128)S(1)}, u32[]{:S(2)}, u32[]{:S(2)}) collective-permute-start(f32[5,1280]{1,0:T(8,128)S(1)} %get-tuple-element.62), channel_id=1, source_target_pairs={{1,0},{2,1},{3,2},{5,4},{6,5},{7,6},{9,8},{10,9},{11,10},{13,12},{... | collective-permute-start | bytes 76808 | tf_op jit(solution)/shard_map/ppermute | solution.py:27
  16.6 6.7 %collective-permute-start.2 = (f32[2,16,1,1280]{3,1,2,0:T(8,128)S(1)}, f32[2,16,1,1280]{3,1,2,0:T(8,128)S(1)}, u32[]{:S(2)}, u32[]{:S(2)}) collective-permute-start(f32[2,16,1,1280]{3,1,2,0:T(8,128)S(1)} %copy.56), channel_id=1, source_target_pairs={{1,0},{2,1},{3,2},{5,4},{6,5},{7,6},{9,8},{10,9},{11,10},{13,12},{... | collective-permute-start | bytes 491528 | tf_op jit(solution)/shard_map/ppermute | solution.py:27
  18.6 5.9 %collective-permute-start.3 = (f32[2,16,1,1280]{3,1,2,0:T(8,128)S(1)}, f32[2,16,1,1280]{3,1,2,0:T(8,128)S(1)}, u32[]{:S(2)}, u32[]{:S(2)}) collective-permute-start(f32[2,16,1,1280]{3,1,2,0:T(8,128)S(1)} %copy.57), channel_id=1, source_target_pairs={{0,1},{1,2},{2,3},{4,5},{5,6},{6,7},{8,9},{9,10},{10,11},{12,13},{... | collective-permute-start | bytes 491528 | tf_op jit(solution)/shard_map/ppermute | solution.py:25
  22.2 0.8 copy-start.4
  22.2 0.8 copy-start.3
  22.3 199.2 %all-gather.5.cloned.1.call-start = ((), (), s32[]{:S(2)}) async-start(), calls=%async_computation.1 | async-start | bytes 2949120 | tf_op jit(solution)/shard_map/all_gather | solution.py:73
  26.3 7.8 %collective-permute-start.4 = (f32[2,16,1,1280]{3,1,2,0:T(8,128)S(1)}, f32[2,16,1,1280]{3,1,2,0:T(8,128)S(1)}, u32[]{:S(2)}, u32[]{:S(2)}) collective-permute-start(f32[2,16,1,1280]{3,1,2,0:T(8,128)S(1)} %copy.28), channel_id=1, source_target_pairs={{1,0},{2,1},{3,2},{5,4},{6,5},{7,6},{9,8},{10,9},{11,10},{13,12},{... | collective-permute-start | bytes 491528 | tf_op jit(solution)/shard_map/ppermute | solution.py:27
  28.3 6.6 %collective-permute-start.5 = (f32[2,16,1,1280]{3,1,2,0:T(8,128)S(1)}, f32[2,16,1,1280]{3,1,2,0:T(8,128)S(1)}, u32[]{:S(2)}, u32[]{:S(2)}) collective-permute-start(f32[2,16,1,1280]{3,1,2,0:T(8,128)S(1)} %copy.30), channel_id=1, source_target_pairs={{0,1},{1,2},{2,3},{4,5},{5,6},{6,7},{8,9},{9,10},{10,11},{12,13},{... | collective-permute-start | bytes 491528 | tf_op jit(solution)/shard_map/ppermute | solution.py:25
  36.7 7.8 %collective-permute-start.6 = (f32[2,16,1,1280]{3,1,2,0:T(8,128)S(1)}, f32[2,16,1,1280]{3,1,2,0:T(8,128)S(1)}, u32[]{:S(2)}, u32[]{:S(2)}) collective-permute-start(f32[2,16,1,1280]{3,1,2,0:T(8,128)S(1)} %copy.32), channel_id=1, source_target_pairs={{1,0},{2,1},{3,2},{5,4},{6,5},{7,6},{9,8},{10,9},{11,10},{13,12},{... | collective-permute-start | bytes 491528 | tf_op jit(solution)/shard_map/ppermute | solution.py:27
  38.7 6.6 %collective-permute-start.7 = (f32[2,16,1,1280]{3,1,2,0:T(8,128)S(1)}, f32[2,16,1,1280]{3,1,2,0:T(8,128)S(1)}, u32[]{:S(2)}, u32[]{:S(2)}) collective-permute-start(f32[2,16,1,1280]{3,1,2,0:T(8,128)S(1)} %copy.34), channel_id=1, source_target_pairs={{0,1},{1,2},{2,3},{4,5},{5,6},{6,7},{8,9},{9,10},{10,11},{12,13},{... | collective-permute-start | bytes 491528 | tf_op jit(solution)/shard_map/ppermute | solution.py:25
  47.2 7.8 %collective-permute-start.8 = (f32[2,16,1,1280]{3,1,2,0:T(8,128)S(1)}, f32[2,16,1,1280]{3,1,2,0:T(8,128)S(1)}, u32[]{:S(2)}, u32[]{:S(2)}) collective-permute-start(f32[2,16,1,1280]{3,1,2,0:T(8,128)S(1)} %copy.36), channel_id=1, source_target_pairs={{1,0},{2,1},{3,2},{5,4},{6,5},{7,6},{9,8},{10,9},{11,10},{13,12},{... | collective-permute-start | bytes 491528 | tf_op jit(solution)/shard_map/ppermute | solution.py:27
  49.1 6.6 %collective-permute-start.9 = (f32[2,16,1,1280]{3,1,2,0:T(8,128)S(1)}, f32[2,16,1,1280]{3,1,2,0:T(8,128)S(1)}, u32[]{:S(2)}, u32[]{:S(2)}) collective-permute-start(f32[2,16,1,1280]{3,1,2,0:T(8,128)S(1)} %copy.38), channel_id=1, source_target_pairs={{0,1},{1,2},{2,3},{4,5},{5,6},{6,7},{8,9},{9,10},{10,11},{12,13},{... | collective-permute-start | bytes 491528 | tf_op jit(solution)/shard_map/ppermute | solution.py:25
  56.0 1.8 copy-start.1
  58.3 64.2 %collective-permute-start.10 = (f32[4,16,8,1280]{3,2,1,0:T(8,128)S(1)}, f32[4,16,8,1280]{3,2,1,0:T(8,128)S(1)}, u32[]{:S(2)}, u32[]{:S(2)}) collective-permute-start(f32[4,16,8,1280]{3,2,1,0:T(8,128)S(1)} %fusion), channel_id=1, source_target_pairs={{0,4},{4,0},{8,12},{12,8},{16,20},{20,16},{24,28},{28,24},{1,5},{5... | collective-permute-start | bytes 7864328 | tf_op jit(solution)/shard_map/ppermute | solution.py:13
  124.4 90.5 %collective-permute-start.11 = (f32[4,16,8,1280]{3,2,1,0:T(8,128)}, f32[4,16,8,1280]{3,2,1,0:T(8,128)}, u32[]{:S(2)}, u32[]{:S(2)}) collective-permute-start(f32[4,16,8,1280]{3,2,1,0:T(8,128)} %add.143), channel_id=1, source_target_pairs={{0,8},{4,12},{8,0},{12,4},{16,24},{20,28},{24,16},{28,20},{1,9},{5... | collective-permute-start | bytes 7864328 | tf_op jit(solution)/shard_map/ppermute | solution.py:13
  219.4 115.3 %collective-permute-start.12 = (f32[4,16,8,1280]{3,2,1,0:T(8,128)}, f32[4,16,8,1280]{3,2,1,0:T(8,128)}, u32[]{:S(2)}, u32[]{:S(2)}) collective-permute-start(f32[4,16,8,1280]{3,2,1,0:T(8,128)} %add.144), channel_id=1, source_target_pairs={{0,16},{4,20},{8,24},{12,28},{16,0},{20,4},{24,8},{28,12},{1,17},{... | collective-permute-start | bytes 7864328 | tf_op jit(solution)/shard_map/ppermute | solution.py:13
  334.6 4.8 %copy-start.2 = (bf16[4,2,16,8,1280]{4,3,2,1,0:T(8,128)(2,1)S(1)}, bf16[4,2,16,8,1280]{4,3,2,1,0:T(8,128)(2,1)}, u32[]{:S(2)}) copy-start(bf16[4,2,16,8,1280]{4,3,2,1,0:T(8,128)(2,1)} %param.7) | copy-start | bytes 7864324
  340.8 6.6 %collective-permute-start.13 = (f32[2,16,1,1280]{3,1,2,0:T(8,128)S(1)}, f32[2,16,1,1280]{3,1,2,0:T(8,128)S(1)}, u32[]{:S(2)}, u32[]{:S(2)}) collective-permute-start(f32[2,16,1,1280]{3,1,2,0:T(8,128)S(1)} %copy.40), channel_id=1, source_target_pairs={{1,0},{2,1},{3,2},{5,4},{6,5},{7,6},{9,8},{10,9},{11,10},{13,12},{... | collective-permute-start | bytes 491528 | tf_op jit(solution)/shard_map/ppermute | solution.py:27
  344.2 4.5 %collective-permute-start.14 = (f32[2,16,1,1280]{3,1,2,0:T(8,128)S(1)}, f32[2,16,1,1280]{3,1,2,0:T(8,128)S(1)}, u32[]{:S(2)}, u32[]{:S(2)}) collective-permute-start(f32[2,16,1,1280]{3,1,2,0:T(8,128)S(1)} %copy.42), channel_id=1, source_target_pairs={{0,1},{1,2},{2,3},{4,5},{5,6},{6,7},{8,9},{9,10},{10,11},{12,13},{... | collective-permute-start | bytes 491528 | tf_op jit(solution)/shard_map/ppermute | solution.py:25
  350.5 7.4 %collective-permute-start.15 = (f32[2,16,1,1280]{3,1,2,0:T(8,128)S(1)}, f32[2,16,1,1280]{3,1,2,0:T(8,128)S(1)}, u32[]{:S(2)}, u32[]{:S(2)}) collective-permute-start(f32[2,16,1,1280]{3,1,2,0:T(8,128)S(1)} %copy.44), channel_id=1, source_target_pairs={{1,0},{2,1},{3,2},{5,4},{6,5},{7,6},{9,8},{10,9},{11,10},{13,12},{... | collective-permute-start | bytes 491528 | tf_op jit(solution)/shard_map/ppermute | solution.py:27
  352.5 6.6 %collective-permute-start.16 = (f32[2,16,1,1280]{3,1,2,0:T(8,128)S(1)}, f32[2,16,1,1280]{3,1,2,0:T(8,128)S(1)}, u32[]{:S(2)}, u32[]{:S(2)}) collective-permute-start(f32[2,16,1,1280]{3,1,2,0:T(8,128)S(1)} %copy.46), channel_id=1, source_target_pairs={{0,1},{1,2},{2,3},{4,5},{5,6},{6,7},{8,9},{9,10},{10,11},{12,13},{... | collective-permute-start | bytes 491528 | tf_op jit(solution)/shard_map/ppermute | solution.py:25
  360.9 7.4 %collective-permute-start.17 = (f32[2,16,1,1280]{3,1,2,0:T(8,128)S(1)}, f32[2,16,1,1280]{3,1,2,0:T(8,128)S(1)}, u32[]{:S(2)}, u32[]{:S(2)}) collective-permute-start(f32[2,16,1,1280]{3,1,2,0:T(8,128)S(1)} %copy.48), channel_id=1, source_target_pairs={{1,0},{2,1},{3,2},{5,4},{6,5},{7,6},{9,8},{10,9},{11,10},{13,12},{... | collective-permute-start | bytes 491528 | tf_op jit(solution)/shard_map/ppermute | solution.py:27
  362.9 6.6 %collective-permute-start.18 = (f32[2,16,1,1280]{3,1,2,0:T(8,128)S(1)}, f32[2,16,1,1280]{3,1,2,0:T(8,128)S(1)}, u32[]{:S(2)}, u32[]{:S(2)}) collective-permute-start(f32[2,16,1,1280]{3,1,2,0:T(8,128)S(1)} %copy.50), channel_id=1, source_target_pairs={{0,1},{1,2},{2,3},{4,5},{5,6},{6,7},{8,9},{9,10},{10,11},{12,13},{... | collective-permute-start | bytes 491528 | tf_op jit(solution)/shard_map/ppermute | solution.py:25
  371.4 7.4 %collective-permute-start.19 = (f32[2,16,1,1280]{3,1,2,0:T(8,128)S(1)}, f32[2,16,1,1280]{3,1,2,0:T(8,128)S(1)}, u32[]{:S(2)}, u32[]{:S(2)}) collective-permute-start(f32[2,16,1,1280]{3,1,2,0:T(8,128)S(1)} %copy.52), channel_id=1, source_target_pairs={{1,0},{2,1},{3,2},{5,4},{6,5},{7,6},{9,8},{10,9},{11,10},{13,12},{... | collective-permute-start | bytes 491528 | tf_op jit(solution)/shard_map/ppermute | solution.py:27
  373.4 6.6 %collective-permute-start.20 = (f32[2,16,1,1280]{3,1,2,0:T(8,128)S(1)}, f32[2,16,1,1280]{3,1,2,0:T(8,128)S(1)}, u32[]{:S(2)}, u32[]{:S(2)}) collective-permute-start(f32[2,16,1,1280]{3,1,2,0:T(8,128)S(1)} %copy.54), channel_id=1, source_target_pairs={{0,1},{1,2},{2,3},{4,5},{5,6},{6,7},{8,9},{9,10},{10,11},{12,13},{... | collective-permute-start | bytes 491528 | tf_op jit(solution)/shard_map/ppermute | solution.py:25
Sparse Core Ops, SparseCore 0:
  22.4 58.7 all-gather.2
  125.8 79.4 all-gather.4
